TPU v7x, 256 devices: a whole 4x4x8 slice. The times are simulated.
256 devices in a mesh: depth: 8 (over x_hi, y), row: 32 (over x_lo, z, core).
Axes of the slice: x: 4 (x_hi: 2, x_lo: 2; x = x_hi * 2 + x_lo), y: 4, z: 8, core: 2. Of those that a mesh axis runs over, the one named last changes fastest.
Arguments:
- index_volume: bfloat16 [8, 512, 2048], P('depth', 'row'), may hold values from -4 to 4
- angles: int32 [2], replicated, may hold values from 0 to 15
- offsets: int32 [8], P('depth'), may hold values from -4 to 4, as said below
- measured: bfloat16 [2, 512, 2048], P(None, 'row'), may hold values from 0 to 2
Outputs:
- gradient: float32 [8, 512, 2048], P('depth', 'row')
Inputs may be any that keep to these rules, and one draw needn't show every extreme that they name: `offsets`: each of -4 and 4 is taken by at least one slice.
All inputs are finite; a program needn't handle non-finite values.
Results may differ from a plain program's by a relative error of at most 0.0003.
Values may be sent and summed in bfloat16 or wider, within the bound.
A program may use at most 64 MiB of HBM per device.

v0:
```python
import math
import jax
import jax.numpy as jnp
from jax import lax
from jax.sharding import PartitionSpec as P

TILTS = 16
HALF = 10
SHIFT = 4
HALFCOL = 64
COLBLK = 128
PHASE_SCALE = 0.5
CHIRP_ROW = 1.3
CHIRP_COL = 1.7


def halo_rows(shard, axis, width):
    size, length = (lax.axis_size(axis), shard.shape[-2])
    up = [(i, i + 1) for i in range(size - 1)]
    down = [(j, i) for i, j in up]
    last = shard[..., length - width :, :]
    initial = shard[..., :width, :]
    before = lax.ppermute(last, axis, up)
    after = lax.ppermute(initial, axis, down)
    return jnp.concatenate([before, shard, after], axis=-2)


def kernel_values(distance, radius, chirp_rate):
    inside = jnp.abs(distance) <= radius
    phase_arg = chirp_rate / radius * distance * distance
    weight = 1.0 / math.sqrt(2 * radius + 1)
    real_part = jnp.where(inside, jnp.cos(phase_arg) * weight, 0.0)
    imag_part = jnp.where(inside, jnp.sin(phase_arg) * weight, 0.0)
    return (real_part, imag_part)


def row_band(offset, height, margin, conjugate):
    extent = (height, height + 2 * margin)
    target = lax.broadcasted_iota(jnp.int32, extent, 0)
    source = lax.broadcasted_iota(jnp.int32, extent, 1)
    offset_used = -offset if conjugate else offset
    distance = (source - target - margin - offset_used).astype(jnp.float32)
    real_part, imag_part = kernel_values(distance, HALF, CHIRP_ROW)
    return (real_part, -imag_part) if conjugate else (real_part, imag_part)


def column_band(conjugate, block_width):
    extent = (block_width + 2 * HALFCOL, block_width)
    source = lax.broadcasted_iota(jnp.int32, extent, 0)
    target = lax.broadcasted_iota(jnp.int32, extent, 1)
    distance = (source - target - HALFCOL).astype(jnp.float32)
    real_part, imag_part = kernel_values(distance, HALFCOL, CHIRP_COL)
    return (real_part, -imag_part) if conjugate else (real_part, imag_part)


def mix_rows(band, extended):

    def product(matrix, operand):
        return jnp.einsum("ij,jc->ic", matrix, operand, precision=lax.Precision.HIGHEST)

    real_part = product(band[0], extended[0]) - product(band[1], extended[1])
    imag_part = product(band[0], extended[1]) + product(band[1], extended[0])
    return jnp.stack([real_part, imag_part], axis=0)


def mix_columns(band, field):
    _, height, columns = field.shape
    blocks = columns // COLBLK
    padded = jnp.pad(field, ((0, 0), (0, 0), (HALFCOL, COLBLK - HALFCOL)))
    middle = padded[..., :columns].reshape(2, height, blocks, COLBLK)
    beyond = padded[..., COLBLK : columns + COLBLK].reshape(2, height, blocks, COLBLK)
    window = jnp.concatenate([middle, beyond], axis=3)

    def product(operand, matrix):
        return jnp.einsum("rbj,ji->rbi", operand, matrix, precision=lax.Precision.HIGH)

    real_part = product(window[0], band[0]) - product(window[1], band[1])
    imag_part = product(window[1], band[0]) + product(window[0], band[1])
    return jnp.stack([real_part, imag_part], axis=0).reshape(2, height, columns)


def rotate(field, cosine, sine):
    real_part = cosine * field[0] - sine * field[1]
    imag_part = cosine * field[1] + sine * field[0]
    return jnp.stack([real_part, imag_part], axis=0)


def plane_wave(angle, row_start, height, columns, total_rows, total_cols):
    across = angle - TILTS // 2
    along = jnp.mod(3 * angle, TILTS) - TILTS // 2
    row_index = row_start + lax.broadcasted_iota(jnp.int32, (height, columns), 0)
    col_index = lax.broadcasted_iota(jnp.int32, (height, columns), 1)
    period = total_cols * total_rows
    cycles_int = jnp.mod(across * col_index * total_rows + along * row_index * total_cols, period)
    phase_arg = 2.0 * math.pi / period * cycles_int.astype(jnp.float32)
    return jnp.stack([jnp.cos(phase_arg), jnp.sin(phase_arg)], axis=0)


def body(index_volume, angles, offsets, measured):
    sections = lax.axis_size("depth")
    section_no = lax.axis_index("depth")
    height = index_volume.shape[1]
    columns = index_volume.shape[2]
    margin = HALF + SHIFT
    row_start = lax.axis_index("row") * height
    total_rows = height * lax.axis_size("row")
    angle_count = angles.shape[0]
    angle_no = section_no % angle_count
    volume = lax.all_gather(index_volume, "depth", axis=0, tiled=True)
    shifts = lax.all_gather(offsets, "depth", axis=0, tiled=True)
    layers = volume.shape[0]
    intensity = lax.dynamic_index_in_dim(measured, angle_no, 0, keepdims=False).astype(jnp.float32)
    angle = lax.dynamic_index_in_dim(angles, angle_no, 0, keepdims=False)
    field = plane_wave(angle, row_start, height, columns, total_rows, columns)
    col_fwd = column_band(False, COLBLK)
    col_adj = column_band(True, COLBLK)
    phases = PHASE_SCALE * volume.astype(jnp.float32)
    cosines = jnp.cos(phases)
    sines = jnp.sin(phases)

    def forward_step(layer_no, carried):
        field, stored = carried
        transmitted = rotate(field, cosines[layer_no], sines[layer_no])
        stored = lax.dynamic_update_index_in_dim(stored, transmitted, layer_no, 0)
        extended = halo_rows(transmitted, "row", margin)
        band = row_band(shifts[layer_no], height, margin, False)
        return (mix_columns(col_fwd, mix_rows(band, extended)), stored)

    stored = jnp.zeros((layers,) + field.shape, jnp.float32)
    field, stored = lax.fori_loop(0, layers, forward_step, (field, stored))
    errors = field[0] * field[0] + field[1] * field[1] - intensity
    adjoint = 2.0 * errors[None] * field

    def backward_step(step, carried):
        adjoint, terms = carried
        layer_no = layers - 1 - step
        returned = mix_columns(col_adj, adjoint)
        extended = halo_rows(returned, "row", margin)
        band = row_band(shifts[layer_no], height, margin, True)
        returned = mix_rows(band, extended)
        transmitted = stored[layer_no]
        term = PHASE_SCALE * (transmitted[0] * returned[1] - transmitted[1] * returned[0])
        terms = lax.dynamic_update_index_in_dim(terms, term, layer_no, 0)
        return (rotate(returned, cosines[layer_no], -sines[layer_no]), terms)

    terms = jnp.zeros((layers, height, columns), jnp.float32)
    adjoint, terms = lax.fori_loop(0, layers, backward_step, (adjoint, terms))
    own = lax.dynamic_index_in_dim(terms, section_no, 0, keepdims=True)
    partner_slice = section_no ^ 1
    for_partner = lax.dynamic_index_in_dim(terms, partner_slice, 0, keepdims=True)
    pairs = [(i, i ^ 1) for i in range(sections)]
    received = lax.ppermute(for_partner, "depth", pairs)
    first = jnp.where(angle_no == 0, own, received)
    second = jnp.where(angle_no == 0, received, own)
    return first + second


def solution(mesh):
    in_specs = (P("depth", "row", None), P(), P("depth"), P(None, "row", None))
    out_specs = P("depth", "row", None)
    return jax.shard_map(body, mesh=mesh, in_specs=in_specs, out_specs=out_specs, check_vma=False)
```

profile of v0, /device:TPU:2, one launch (start us, length us, event | category | flops | bytes accessed | tf_op | source)
XLA Modules:
  0.0 368.7 jit_solution(4456685893062569715)
XLA Ops:
  3.0 1.3 dynamic-slice
  5.0 12.8 %all-reduce.2 = s32[8]{0:T(128)S(1)} all-reduce(s32[8]{0:T(128)S(1)} %dynamic-update-slice), channel_id=1, replica_groups=mesh['depth'=8,'row'=32] {'depth'}, use_global_device_ids=true, to_apply=%add.2 | all-reduce | flops 8 | bytes 64
  17.7 35.1 %all_gather.7 = bf16[8,16,2048]{2,1,0:T(8,128)(2,1)S(1)} all-gather(bf16[1,16,2048]{2,1,0:T(8,128)(2,1)} %param.8), channel_id=1, replica_groups=mesh['depth'=8,'row'=32] {'depth'}, dimensions={0}, use_global_device_ids=true | all-gather | bytes 589824 | tf_op jit(solution)/shard_map/all_gather | solution.py:109
  52.8 3.7 %fusion.193 = (f32[8,16,2048]{2,1,0:T(8,128)S(1)}, f32[8,16,2048]{2,1,0:T(8,128)S(1)}) fusion(bf16[8,16,2048]{2,1,0:T(8,128)(2,1)S(1)} %all_gather.7), kind=kLoop, calls=%fused_computation.255 | loop fusion | flops 524288 | bytes 2621440 | tf_op jit(solution)/shard_map/sin | solution.py:119
  57.2 155.0 %while.38 = (s32[]{:T(128)}, f32[2,16,2048]{2,1,0:T(8,128)S(1)}, f32[8,2,16,2048]{3,2,1,0:T(8,128)}, s32[8]{0:T(128)S(1)}, f32[8,16,2048]{2,1,0:T(8,128)S(1)}, /*index=5*/f32[8,16,2048]{2,1,0:T(8,128)S(1)}, s32[]{:T(128)}) while((s32[]{:T(128)}, f32[2,16,2048]{2,1,0:T(8,128)S(1)}, f32[8,2,16,2048]{3,2,1,0:T(8,128)}, ...), condition=%wide.region_1.2_spmd.clone.clone, body=%wide.region_0.1_spmd.clone.clone.sunk | while | flops 273272320 | bytes 14237897 | solution.py:130
  57.3 1.9 collective-permute-start
  59.2 2.4 collective-permute-start.1
  63.1 8.9 %collective-permute-done.1 = f32[2,14,2048]{2,1,0:T(8,128)S(1)} collective-permute-done((f32[2,14,2048]{2,1,0:T(8,128)S(1)}, f32[2,14,2048]{2,1,0:T(8,128)S(1)}, u32[]{:S(2)}, u32[]{:S(2)}) %collective-permute-start.1) | collective-permute-done | bytes 229408 | tf_op jit(solution)/shard_map/while/body/eval_jaxpr/ppermute | solution.py:23
  79.3 1.9 collective-permute-start
  81.2 2.4 collective-permute-start.1
  85.1 5.9 %collective-permute-done.1 = f32[2,14,2048]{2,1,0:T(8,128)S(1)} collective-permute-done((f32[2,14,2048]{2,1,0:T(8,128)S(1)}, f32[2,14,2048]{2,1,0:T(8,128)S(1)}, u32[]{:S(2)}, u32[]{:S(2)}) %collective-permute-start.1) | collective-permute-done | bytes 229408 | tf_op jit(solution)/shard_map/while/body/eval_jaxpr/ppermute | solution.py:23
  98.3 1.9 collective-permute-start
  100.2 2.4 collective-permute-start.1
  104.1 5.9 %collective-permute-done.1 = f32[2,14,2048]{2,1,0:T(8,128)S(1)} collective-permute-done((f32[2,14,2048]{2,1,0:T(8,128)S(1)}, f32[2,14,2048]{2,1,0:T(8,128)S(1)}, u32[]{:S(2)}, u32[]{:S(2)}) %collective-permute-start.1) | collective-permute-done | bytes 229408 | tf_op jit(solution)/shard_map/while/body/eval_jaxpr/ppermute | solution.py:23
  117.3 1.9 collective-permute-start
  119.2 2.4 collective-permute-start.1
  123.1 5.9 %collective-permute-done.1 = f32[2,14,2048]{2,1,0:T(8,128)S(1)} collective-permute-done((f32[2,14,2048]{2,1,0:T(8,128)S(1)}, f32[2,14,2048]{2,1,0:T(8,128)S(1)}, u32[]{:S(2)}, u32[]{:S(2)}) %collective-permute-start.1) | collective-permute-done | bytes 229408 | tf_op jit(solution)/shard_map/while/body/eval_jaxpr/ppermute | solution.py:23
  136.3 1.9 collective-permute-start
  138.2 2.4 collective-permute-start.1
  142.1 5.9 %collective-permute-done.1 = f32[2,14,2048]{2,1,0:T(8,128)S(1)} collective-permute-done((f32[2,14,2048]{2,1,0:T(8,128)S(1)}, f32[2,14,2048]{2,1,0:T(8,128)S(1)}, u32[]{:S(2)}, u32[]{:S(2)}) %collective-permute-start.1) | collective-permute-done | bytes 229408 | tf_op jit(solution)/shard_map/while/body/eval_jaxpr/ppermute | solution.py:23
  155.3 1.9 collective-permute-start
  157.2 2.4 collective-permute-start.1
  161.1 5.9 %collective-permute-done.1 = f32[2,14,2048]{2,1,0:T(8,128)S(1)} collective-permute-done((f32[2,14,2048]{2,1,0:T(8,128)S(1)}, f32[2,14,2048]{2,1,0:T(8,128)S(1)}, u32[]{:S(2)}, u32[]{:S(2)}) %collective-permute-start.1) | collective-permute-done | bytes 229408 | tf_op jit(solution)/shard_map/while/body/eval_jaxpr/ppermute | solution.py:23
  174.3 1.9 collective-permute-start
  176.2 2.4 collective-permute-start.1
  180.1 5.9 %collective-permute-done.1 = f32[2,14,2048]{2,1,0:T(8,128)S(1)} collective-permute-done((f32[2,14,2048]{2,1,0:T(8,128)S(1)}, f32[2,14,2048]{2,1,0:T(8,128)S(1)}, u32[]{:S(2)}, u32[]{:S(2)}) %collective-permute-start.1) | collective-permute-done | bytes 229408 | tf_op jit(solution)/shard_map/while/body/eval_jaxpr/ppermute | solution.py:23
  193.3 1.9 collective-permute-start
  195.2 2.4 collective-permute-start.1
  199.1 5.9 %collective-permute-done.1 = f32[2,14,2048]{2,1,0:T(8,128)S(1)} collective-permute-done((f32[2,14,2048]{2,1,0:T(8,128)S(1)}, f32[2,14,2048]{2,1,0:T(8,128)S(1)}, u32[]{:S(2)}, u32[]{:S(2)}) %collective-permute-start.1) | collective-permute-done | bytes 229408 | tf_op jit(solution)/shard_map/while/body/eval_jaxpr/ppermute | solution.py:23
  213.3 147.8 %while.39 = (s32[]{:T(128)}, f32[2,16,2048]{2,1,0:T(8,128)S(1)}, f32[8,16,2048]{2,1,0:T(8,128)}, f32[8,16,2048]{2,1,0:T(8,128)S(1)}, s32[8]{0:T(128)S(1)}, /*ind...) while((s32[]{:T(128)}, f32[2,16,2048]{2,1,0:T(8,128)S(1)}, ...), condition=%wide.region_3.4_spmd.clone.clone, body=%wide.region_2.3_spmd.clone.clone.sunk | while | flops 272724864 | bytes 14156587 | solution.py:147
  216.8 1.9 collective-permute-start.2
  218.8 2.4 collective-permute-start.3
  222.6 5.9 %collective-permute-done.3 = f32[2,14,2048]{2,1,0:T(8,128)S(1)} collective-permute-done((f32[2,14,2048]{2,1,0:T(8,128)S(1)}, f32[2,14,2048]{2,1,0:T(8,128)S(1)}, u32[]{:S(2)}, u32[]{:S(2)}) %collective-permute-start.3) | collective-permute-done | bytes 229408 | tf_op jit(solution)/shard_map/while/body/eval_jaxpr/ppermute | solution.py:23
  229.7 2.0 fusion.248
  235.3 1.9 collective-permute-start.2
  237.2 2.4 collective-permute-start.3
  241.1 5.9 %collective-permute-done.3 = f32[2,14,2048]{2,1,0:T(8,128)S(1)} collective-permute-done((f32[2,14,2048]{2,1,0:T(8,128)S(1)}, f32[2,14,2048]{2,1,0:T(8,128)S(1)}, u32[]{:S(2)}, u32[]{:S(2)}) %collective-permute-start.3) | collective-permute-done | bytes 229408 | tf_op jit(solution)/shard_map/while/body/eval_jaxpr/ppermute | solution.py:23
  248.2 2.0 fusion.248
  253.8 1.9 collective-permute-start.2
  255.7 2.4 collective-permute-start.3
  259.6 5.9 %collective-permute-done.3 = f32[2,14,2048]{2,1,0:T(8,128)S(1)} collective-permute-done((f32[2,14,2048]{2,1,0:T(8,128)S(1)}, f32[2,14,2048]{2,1,0:T(8,128)S(1)}, u32[]{:S(2)}, u32[]{:S(2)}) %collective-permute-start.3) | collective-permute-done | bytes 229408 | tf_op jit(solution)/shard_map/while/body/eval_jaxpr/ppermute | solution.py:23
  266.7 2.0 fusion.248
  272.3 1.9 collective-permute-start.2
  274.2 2.4 collective-permute-start.3
  278.1 5.9 %collective-permute-done.3 = f32[2,14,2048]{2,1,0:T(8,128)S(1)} collective-permute-done((f32[2,14,2048]{2,1,0:T(8,128)S(1)}, f32[2,14,2048]{2,1,0:T(8,128)S(1)}, u32[]{:S(2)}, u32[]{:S(2)}) %collective-permute-start.3) | collective-permute-done | bytes 229408 | tf_op jit(solution)/shard_map/while/body/eval_jaxpr/ppermute | solution.py:23
  285.2 2.0 fusion.248
  290.7 1.9 collective-permute-start.2
  292.7 2.4 collective-permute-start.3
  296.5 5.9 %collective-permute-done.3 = f32[2,14,2048]{2,1,0:T(8,128)S(1)} collective-permute-done((f32[2,14,2048]{2,1,0:T(8,128)S(1)}, f32[2,14,2048]{2,1,0:T(8,128)S(1)}, u32[]{:S(2)}, u32[]{:S(2)}) %collective-permute-start.3) | collective-permute-done | bytes 229408 | tf_op jit(solution)/shard_map/while/body/eval_jaxpr/ppermute | solution.py:23
  303.6 2.0 fusion.248
  309.2 1.9 collective-permute-start.2
  311.2 2.4 collective-permute-start.3
  315.0 5.9 %collective-permute-done.3 = f32[2,14,2048]{2,1,0:T(8,128)S(1)} collective-permute-done((f32[2,14,2048]{2,1,0:T(8,128)S(1)}, f32[2,14,2048]{2,1,0:T(8,128)S(1)}, u32[]{:S(2)}, u32[]{:S(2)}) %collective-permute-start.3) | collective-permute-done | bytes 229408 | tf_op jit(solution)/shard_map/while/body/eval_jaxpr/ppermute | solution.py:23
  322.1 2.0 fusion.248
  327.7 1.9 collective-permute-start.2
  329.6 2.4 collective-permute-start.3
  333.5 5.9 %collective-permute-done.3 = f32[2,14,2048]{2,1,0:T(8,128)S(1)} collective-permute-done((f32[2,14,2048]{2,1,0:T(8,128)S(1)}, f32[2,14,2048]{2,1,0:T(8,128)S(1)}, u32[]{:S(2)}, u32[]{:S(2)}) %collective-permute-start.3) | collective-permute-done | bytes 229408 | tf_op jit(solution)/shard_map/while/body/eval_jaxpr/ppermute | solution.py:23
  340.6 2.0 fusion.248
  346.2 1.9 collective-permute-start.2
  348.1 2.4 collective-permute-start.3
  352.0 5.9 %collective-permute-done.3 = f32[2,14,2048]{2,1,0:T(8,128)S(1)} collective-permute-done((f32[2,14,2048]{2,1,0:T(8,128)S(1)}, f32[2,14,2048]{2,1,0:T(8,128)S(1)}, u32[]{:S(2)}, u32[]{:S(2)}) %collective-permute-start.3) | collective-permute-done | bytes 229408 | tf_op jit(solution)/shard_map/while/body/eval_jaxpr/ppermute | solution.py:23
  359.0 2.0 fusion.248
  362.1 4.9 %collective-permute-done.4 = f32[1,16,2048]{2,1,0:T(8,128)S(1)} collective-permute-done((f32[1,16,2048]{2,1,0:T(8,128)S(1)}, f32[1,16,2048]{2,1,0:T(8,128)S(1)}, u32[]{:S(2)}, u32[]{:S(2)}) %collective-permute-start.4) | collective-permute-done | bytes 131104 | tf_op jit(solution)/shard_map/ppermute | solution.py:152
  367.1 1.6 select_add_fusion
  (375 shorter events, 116.5 us)
Async XLA Ops:
  57.1 155.0 %copy-start = (bf16[2,16,2048]{2,1,0:T(8,128)(2,1)S(1)}, bf16[2,16,2048]{2,1,0:T(8,128)(2,1)}, u32[]{:S(2)}) copy-start(bf16[2,16,2048]{2,1,0:T(8,128)(2,1)} %param.11) | copy-start | bytes 393220
  57.3 5.8 %collective-permute-start = (f32[2,14,2048]{2,1,0:T(8,128)S(1)}, f32[2,14,2048]{2,1,0:T(8,128)S(1)}, u32[]{:S(2)}, u32[]{:S(2)}) collective-permute-start(f32[2,14,2048]{2,1,0:T(8,128)S(1)} %get-tuple-element.655), channel_id=1, source_target_pairs={{1,0},{2,1},{3,2},{4,3},{5,4},{6,5},{7,6},{8,7},{9,8},{10,9},{11,1... | collective-permute-start | bytes 688136 | tf_op jit(solution)/shard_map/while/body/eval_jaxpr/ppermute | solution.py:24
  59.2 12.8 %collective-permute-start.1 = (f32[2,14,2048]{2,1,0:T(8,128)S(1)}, f32[2,14,2048]{2,1,0:T(8,128)S(1)}, u32[]{:S(2)}, u32[]{:S(2)}) collective-permute-start(f32[2,14,2048]{2,1,0:T(8,128)S(1)} %get-tuple-element.656), channel_id=1, source_target_pairs={{0,1},{1,2},{2,3},{3,4},{4,5},{5,6},{6,7},{7,8},{8,9},{9,10},{10,1... | collective-permute-start | bytes 688136 | tf_op jit(solution)/shard_map/while/body/eval_jaxpr/ppermute | solution.py:23
  79.3 5.8 %collective-permute-start = (f32[2,14,2048]{2,1,0:T(8,128)S(1)}, f32[2,14,2048]{2,1,0:T(8,128)S(1)}, u32[]{:S(2)}, u32[]{:S(2)}) collective-permute-start(f32[2,14,2048]{2,1,0:T(8,128)S(1)} %get-tuple-element.655), channel_id=1, source_target_pairs={{1,0},{2,1},{3,2},{4,3},{5,4},{6,5},{7,6},{8,7},{9,8},{10,9},{11,1... | collective-permute-start | bytes 688136 | tf_op jit(solution)/shard_map/while/body/eval_jaxpr/ppermute | solution.py:24
  81.2 9.8 %collective-permute-start.1 = (f32[2,14,2048]{2,1,0:T(8,128)S(1)}, f32[2,14,2048]{2,1,0:T(8,128)S(1)}, u32[]{:S(2)}, u32[]{:S(2)}) collective-permute-start(f32[2,14,2048]{2,1,0:T(8,128)S(1)} %get-tuple-element.656), channel_id=1, source_target_pairs={{0,1},{1,2},{2,3},{3,4},{4,5},{5,6},{6,7},{7,8},{8,9},{9,10},{10,1... | collective-permute-start | bytes 688136 | tf_op jit(solution)/shard_map/while/body/eval_jaxpr/ppermute | solution.py:23
  98.3 5.8 %collective-permute-start = (f32[2,14,2048]{2,1,0:T(8,128)S(1)}, f32[2,14,2048]{2,1,0:T(8,128)S(1)}, u32[]{:S(2)}, u32[]{:S(2)}) collective-permute-start(f32[2,14,2048]{2,1,0:T(8,128)S(1)} %get-tuple-element.655), channel_id=1, source_target_pairs={{1,0},{2,1},{3,2},{4,3},{5,4},{6,5},{7,6},{8,7},{9,8},{10,9},{11,1... | collective-permute-start | bytes 688136 | tf_op jit(solution)/shard_map/while/body/eval_jaxpr/ppermute | solution.py:24
  100.2 9.8 %collective-permute-start.1 = (f32[2,14,2048]{2,1,0:T(8,128)S(1)}, f32[2,14,2048]{2,1,0:T(8,128)S(1)}, u32[]{:S(2)}, u32[]{:S(2)}) collective-permute-start(f32[2,14,2048]{2,1,0:T(8,128)S(1)} %get-tuple-element.656), channel_id=1, source_target_pairs={{0,1},{1,2},{2,3},{3,4},{4,5},{5,6},{6,7},{7,8},{8,9},{9,10},{10,1... | collective-permute-start | bytes 688136 | tf_op jit(solution)/shard_map/while/body/eval_jaxpr/ppermute | solution.py:23
  117.3 5.8 %collective-permute-start = (f32[2,14,2048]{2,1,0:T(8,128)S(1)}, f32[2,14,2048]{2,1,0:T(8,128)S(1)}, u32[]{:S(2)}, u32[]{:S(2)}) collective-permute-start(f32[2,14,2048]{2,1,0:T(8,128)S(1)} %get-tuple-element.655), channel_id=1, source_target_pairs={{1,0},{2,1},{3,2},{4,3},{5,4},{6,5},{7,6},{8,7},{9,8},{10,9},{11,1... | collective-permute-start | bytes 688136 | tf_op jit(solution)/shard_map/while/body/eval_jaxpr/ppermute | solution.py:24
  119.2 9.8 %collective-permute-start.1 = (f32[2,14,2048]{2,1,0:T(8,128)S(1)}, f32[2,14,2048]{2,1,0:T(8,128)S(1)}, u32[]{:S(2)}, u32[]{:S(2)}) collective-permute-start(f32[2,14,2048]{2,1,0:T(8,128)S(1)} %get-tuple-element.656), channel_id=1, source_target_pairs={{0,1},{1,2},{2,3},{3,4},{4,5},{5,6},{6,7},{7,8},{8,9},{9,10},{10,1... | collective-permute-start | bytes 688136 | tf_op jit(solution)/shard_map/while/body/eval_jaxpr/ppermute | solution.py:23
  136.3 5.8 %collective-permute-start = (f32[2,14,2048]{2,1,0:T(8,128)S(1)}, f32[2,14,2048]{2,1,0:T(8,128)S(1)}, u32[]{:S(2)}, u32[]{:S(2)}) collective-permute-start(f32[2,14,2048]{2,1,0:T(8,128)S(1)} %get-tuple-element.655), channel_id=1, source_target_pairs={{1,0},{2,1},{3,2},{4,3},{5,4},{6,5},{7,6},{8,7},{9,8},{10,9},{11,1... | collective-permute-start | bytes 688136 | tf_op jit(solution)/shard_map/while/body/eval_jaxpr/ppermute | solution.py:24
  138.2 9.8 %collective-permute-start.1 = (f32[2,14,2048]{2,1,0:T(8,128)S(1)}, f32[2,14,2048]{2,1,0:T(8,128)S(1)}, u32[]{:S(2)}, u32[]{:S(2)}) collective-permute-start(f32[2,14,2048]{2,1,0:T(8,128)S(1)} %get-tuple-element.656), channel_id=1, source_target_pairs={{0,1},{1,2},{2,3},{3,4},{4,5},{5,6},{6,7},{7,8},{8,9},{9,10},{10,1... | collective-permute-start | bytes 688136 | tf_op jit(solution)/shard_map/while/body/eval_jaxpr/ppermute | solution.py:23
  155.3 5.8 %collective-permute-start = (f32[2,14,2048]{2,1,0:T(8,128)S(1)}, f32[2,14,2048]{2,1,0:T(8,128)S(1)}, u32[]{:S(2)}, u32[]{:S(2)}) collective-permute-start(f32[2,14,2048]{2,1,0:T(8,128)S(1)} %get-tuple-element.655), channel_id=1, source_target_pairs={{1,0},{2,1},{3,2},{4,3},{5,4},{6,5},{7,6},{8,7},{9,8},{10,9},{11,1... | collective-permute-start | bytes 688136 | tf_op jit(solution)/shard_map/while/body/eval_jaxpr/ppermute | solution.py:24
  157.2 9.8 %collective-permute-start.1 = (f32[2,14,2048]{2,1,0:T(8,128)S(1)}, f32[2,14,2048]{2,1,0:T(8,128)S(1)}, u32[]{:S(2)}, u32[]{:S(2)}) collective-permute-start(f32[2,14,2048]{2,1,0:T(8,128)S(1)} %get-tuple-element.656), channel_id=1, source_target_pairs={{0,1},{1,2},{2,3},{3,4},{4,5},{5,6},{6,7},{7,8},{8,9},{9,10},{10,1... | collective-permute-start | bytes 688136 | tf_op jit(solution)/shard_map/while/body/eval_jaxpr/ppermute | solution.py:23
  174.3 5.8 %collective-permute-start = (f32[2,14,2048]{2,1,0:T(8,128)S(1)}, f32[2,14,2048]{2,1,0:T(8,128)S(1)}, u32[]{:S(2)}, u32[]{:S(2)}) collective-permute-start(f32[2,14,2048]{2,1,0:T(8,128)S(1)} %get-tuple-element.655), channel_id=1, source_target_pairs={{1,0},{2,1},{3,2},{4,3},{5,4},{6,5},{7,6},{8,7},{9,8},{10,9},{11,1... | collective-permute-start | bytes 688136 | tf_op jit(solution)/shard_map/while/body/eval_jaxpr/ppermute | solution.py:24
  176.2 9.8 %collective-permute-start.1 = (f32[2,14,2048]{2,1,0:T(8,128)S(1)}, f32[2,14,2048]{2,1,0:T(8,128)S(1)}, u32[]{:S(2)}, u32[]{:S(2)}) collective-permute-start(f32[2,14,2048]{2,1,0:T(8,128)S(1)} %get-tuple-element.656), channel_id=1, source_target_pairs={{0,1},{1,2},{2,3},{3,4},{4,5},{5,6},{6,7},{7,8},{8,9},{9,10},{10,1... | collective-permute-start | bytes 688136 | tf_op jit(solution)/shard_map/while/body/eval_jaxpr/ppermute | solution.py:23
  193.3 5.8 %collective-permute-start = (f32[2,14,2048]{2,1,0:T(8,128)S(1)}, f32[2,14,2048]{2,1,0:T(8,128)S(1)}, u32[]{:S(2)}, u32[]{:S(2)}) collective-permute-start(f32[2,14,2048]{2,1,0:T(8,128)S(1)} %get-tuple-element.655), channel_id=1, source_target_pairs={{1,0},{2,1},{3,2},{4,3},{5,4},{6,5},{7,6},{8,7},{9,8},{10,9},{11,1... | collective-permute-start | bytes 688136 | tf_op jit(solution)/shard_map/while/body/eval_jaxpr/ppermute | solution.py:24
  195.2 9.8 %collective-permute-start.1 = (f32[2,14,2048]{2,1,0:T(8,128)S(1)}, f32[2,14,2048]{2,1,0:T(8,128)S(1)}, u32[]{:S(2)}, u32[]{:S(2)}) collective-permute-start(f32[2,14,2048]{2,1,0:T(8,128)S(1)} %get-tuple-element.656), channel_id=1, source_target_pairs={{0,1},{1,2},{2,3},{3,4},{4,5},{5,6},{6,7},{7,8},{8,9},{9,10},{10,1... | collective-permute-start | bytes 688136 | tf_op jit(solution)/shard_map/while/body/eval_jaxpr/ppermute | solution.py:23
  216.8 5.8 %collective-permute-start.2 = (f32[2,14,2048]{2,1,0:T(8,128)S(1)}, f32[2,14,2048]{2,1,0:T(8,128)S(1)}, u32[]{:S(2)}, u32[]{:S(2)}) collective-permute-start(f32[2,14,2048]{2,1,0:T(8,128)S(1)} %get-tuple-element.668), channel_id=1, source_target_pairs={{1,0},{2,1},{3,2},{4,3},{5,4},{6,5},{7,6},{8,7},{9,8},{10,9},{11,1... | collective-permute-start | bytes 688136 | tf_op jit(solution)/shard_map/while/body/eval_jaxpr/ppermute | solution.py:24
  218.8 9.8 %collective-permute-start.3 = (f32[2,14,2048]{2,1,0:T(8,128)S(1)}, f32[2,14,2048]{2,1,0:T(8,128)S(1)}, u32[]{:S(2)}, u32[]{:S(2)}) collective-permute-start(f32[2,14,2048]{2,1,0:T(8,128)S(1)} %get-tuple-element.669), channel_id=1, source_target_pairs={{0,1},{1,2},{2,3},{3,4},{4,5},{5,6},{6,7},{7,8},{8,9},{9,10},{10,1... | collective-permute-start | bytes 688136 | tf_op jit(solution)/shard_map/while/body/eval_jaxpr/ppermute | solution.py:23
  235.3 5.8 %collective-permute-start.2 = (f32[2,14,2048]{2,1,0:T(8,128)S(1)}, f32[2,14,2048]{2,1,0:T(8,128)S(1)}, u32[]{:S(2)}, u32[]{:S(2)}) collective-permute-start(f32[2,14,2048]{2,1,0:T(8,128)S(1)} %get-tuple-element.668), channel_id=1, source_target_pairs={{1,0},{2,1},{3,2},{4,3},{5,4},{6,5},{7,6},{8,7},{9,8},{10,9},{11,1... | collective-permute-start | bytes 688136 | tf_op jit(solution)/shard_map/while/body/eval_jaxpr/ppermute | solution.py:24
  237.2 9.8 %collective-permute-start.3 = (f32[2,14,2048]{2,1,0:T(8,128)S(1)}, f32[2,14,2048]{2,1,0:T(8,128)S(1)}, u32[]{:S(2)}, u32[]{:S(2)}) collective-permute-start(f32[2,14,2048]{2,1,0:T(8,128)S(1)} %get-tuple-element.669), channel_id=1, source_target_pairs={{0,1},{1,2},{2,3},{3,4},{4,5},{5,6},{6,7},{7,8},{8,9},{9,10},{10,1... | collective-permute-start | bytes 688136 | tf_op jit(solution)/shard_map/while/body/eval_jaxpr/ppermute | solution.py:23
  253.8 5.8 %collective-permute-start.2 = (f32[2,14,2048]{2,1,0:T(8,128)S(1)}, f32[2,14,2048]{2,1,0:T(8,128)S(1)}, u32[]{:S(2)}, u32[]{:S(2)}) collective-permute-start(f32[2,14,2048]{2,1,0:T(8,128)S(1)} %get-tuple-element.668), channel_id=1, source_target_pairs={{1,0},{2,1},{3,2},{4,3},{5,4},{6,5},{7,6},{8,7},{9,8},{10,9},{11,1... | collective-permute-start | bytes 688136 | tf_op jit(solution)/shard_map/while/body/eval_jaxpr/ppermute | solution.py:24
  255.7 9.8 %collective-permute-start.3 = (f32[2,14,2048]{2,1,0:T(8,128)S(1)}, f32[2,14,2048]{2,1,0:T(8,128)S(1)}, u32[]{:S(2)}, u32[]{:S(2)}) collective-permute-start(f32[2,14,2048]{2,1,0:T(8,128)S(1)} %get-tuple-element.669), channel_id=1, source_target_pairs={{0,1},{1,2},{2,3},{3,4},{4,5},{5,6},{6,7},{7,8},{8,9},{9,10},{10,1... | collective-permute-start | bytes 688136 | tf_op jit(solution)/shard_map/while/body/eval_jaxpr/ppermute | solution.py:23
  272.3 5.8 %collective-permute-start.2 = (f32[2,14,2048]{2,1,0:T(8,128)S(1)}, f32[2,14,2048]{2,1,0:T(8,128)S(1)}, u32[]{:S(2)}, u32[]{:S(2)}) collective-permute-start(f32[2,14,2048]{2,1,0:T(8,128)S(1)} %get-tuple-element.668), channel_id=1, source_target_pairs={{1,0},{2,1},{3,2},{4,3},{5,4},{6,5},{7,6},{8,7},{9,8},{10,9},{11,1... | collective-permute-start | bytes 688136 | tf_op jit(solution)/shard_map/while/body/eval_jaxpr/ppermute | solution.py:24
  274.2 9.8 %collective-permute-start.3 = (f32[2,14,2048]{2,1,0:T(8,128)S(1)}, f32[2,14,2048]{2,1,0:T(8,128)S(1)}, u32[]{:S(2)}, u32[]{:S(2)}) collective-permute-start(f32[2,14,2048]{2,1,0:T(8,128)S(1)} %get-tuple-element.669), channel_id=1, source_target_pairs={{0,1},{1,2},{2,3},{3,4},{4,5},{5,6},{6,7},{7,8},{8,9},{9,10},{10,1... | collective-permute-start | bytes 688136 | tf_op jit(solution)/shard_map/while/body/eval_jaxpr/ppermute | solution.py:23
  290.7 5.8 %collective-permute-start.2 = (f32[2,14,2048]{2,1,0:T(8,128)S(1)}, f32[2,14,2048]{2,1,0:T(8,128)S(1)}, u32[]{:S(2)}, u32[]{:S(2)}) collective-permute-start(f32[2,14,2048]{2,1,0:T(8,128)S(1)} %get-tuple-element.668), channel_id=1, source_target_pairs={{1,0},{2,1},{3,2},{4,3},{5,4},{6,5},{7,6},{8,7},{9,8},{10,9},{11,1... | collective-permute-start | bytes 688136 | tf_op jit(solution)/shard_map/while/body/eval_jaxpr/ppermute | solution.py:24
  292.7 9.8 %collective-permute-start.3 = (f32[2,14,2048]{2,1,0:T(8,128)S(1)}, f32[2,14,2048]{2,1,0:T(8,128)S(1)}, u32[]{:S(2)}, u32[]{:S(2)}) collective-permute-start(f32[2,14,2048]{2,1,0:T(8,128)S(1)} %get-tuple-element.669), channel_id=1, source_target_pairs={{0,1},{1,2},{2,3},{3,4},{4,5},{5,6},{6,7},{7,8},{8,9},{9,10},{10,1... | collective-permute-start | bytes 688136 | tf_op jit(solution)/shard_map/while/body/eval_jaxpr/ppermute | solution.py:23
  309.2 5.8 %collective-permute-start.2 = (f32[2,14,2048]{2,1,0:T(8,128)S(1)}, f32[2,14,2048]{2,1,0:T(8,128)S(1)}, u32[]{:S(2)}, u32[]{:S(2)}) collective-permute-start(f32[2,14,2048]{2,1,0:T(8,128)S(1)} %get-tuple-element.668), channel_id=1, source_target_pairs={{1,0},{2,1},{3,2},{4,3},{5,4},{6,5},{7,6},{8,7},{9,8},{10,9},{11,1... | collective-permute-start | bytes 688136 | tf_op jit(solution)/shard_map/while/body/eval_jaxpr/ppermute | solution.py:24
  311.2 9.8 %collective-permute-start.3 = (f32[2,14,2048]{2,1,0:T(8,128)S(1)}, f32[2,14,2048]{2,1,0:T(8,128)S(1)}, u32[]{:S(2)}, u32[]{:S(2)}) collective-permute-start(f32[2,14,2048]{2,1,0:T(8,128)S(1)} %get-tuple-element.669), channel_id=1, source_target_pairs={{0,1},{1,2},{2,3},{3,4},{4,5},{5,6},{6,7},{7,8},{8,9},{9,10},{10,1... | collective-permute-start | bytes 688136 | tf_op jit(solution)/shard_map/while/body/eval_jaxpr/ppermute | solution.py:23
  327.7 5.8 %collective-permute-start.2 = (f32[2,14,2048]{2,1,0:T(8,128)S(1)}, f32[2,14,2048]{2,1,0:T(8,128)S(1)}, u32[]{:S(2)}, u32[]{:S(2)}) collective-permute-start(f32[2,14,2048]{2,1,0:T(8,128)S(1)} %get-tuple-element.668), channel_id=1, source_target_pairs={{1,0},{2,1},{3,2},{4,3},{5,4},{6,5},{7,6},{8,7},{9,8},{10,9},{11,1... | collective-permute-start | bytes 688136 | tf_op jit(solution)/shard_map/while/body/eval_jaxpr/ppermute | solution.py:24
  329.6 9.8 %collective-permute-start.3 = (f32[2,14,2048]{2,1,0:T(8,128)S(1)}, f32[2,14,2048]{2,1,0:T(8,128)S(1)}, u32[]{:S(2)}, u32[]{:S(2)}) collective-permute-start(f32[2,14,2048]{2,1,0:T(8,128)S(1)} %get-tuple-element.669), channel_id=1, source_target_pairs={{0,1},{1,2},{2,3},{3,4},{4,5},{5,6},{6,7},{7,8},{8,9},{9,10},{10,1... | collective-permute-start | bytes 688136 | tf_op jit(solution)/shard_map/while/body/eval_jaxpr/ppermute | solution.py:23
  346.2 5.8 %collective-permute-start.2 = (f32[2,14,2048]{2,1,0:T(8,128)S(1)}, f32[2,14,2048]{2,1,0:T(8,128)S(1)}, u32[]{:S(2)}, u32[]{:S(2)}) collective-permute-start(f32[2,14,2048]{2,1,0:T(8,128)S(1)} %get-tuple-element.668), channel_id=1, source_target_pairs={{1,0},{2,1},{3,2},{4,3},{5,4},{6,5},{7,6},{8,7},{9,8},{10,9},{11,1... | collective-permute-start | bytes 688136 | tf_op jit(solution)/shard_map/while/body/eval_jaxpr/ppermute | solution.py:24
  348.1 9.8 %collective-permute-start.3 = (f32[2,14,2048]{2,1,0:T(8,128)S(1)}, f32[2,14,2048]{2,1,0:T(8,128)S(1)}, u32[]{:S(2)}, u32[]{:S(2)}) collective-permute-start(f32[2,14,2048]{2,1,0:T(8,128)S(1)} %get-tuple-element.669), channel_id=1, source_target_pairs={{0,1},{1,2},{2,3},{3,4},{4,5},{5,6},{6,7},{7,8},{8,9},{9,10},{10,1... | collective-permute-start | bytes 688136 | tf_op jit(solution)/shard_map/while/body/eval_jaxpr/ppermute | solution.py:23
  362.0 5.1 %collective-permute-start.4 = (f32[1,16,2048]{2,1,0:T(8,128)S(1)}, f32[1,16,2048]{2,1,0:T(8,128)S(1)}, u32[]{:S(2)}, u32[]{:S(2)}) collective-permute-start(f32[1,16,2048]{2,1,0:T(8,128)S(1)} %constant_dynamic-slice_fusion), channel_id=1, source_target_pairs={{0,32},{32,0},{64,96},{96,64},{128,160},{160,128},{192,224},{224,1... | collective-permute-start | bytes 393224 | tf_op jit(solution)/shard_map/ppermute | solution.py:152
where the time goes:
time: 370 us; the launch traced here: 369 us
  waiting for transfers between devices  105 us (28%)
  matrix products  100 us (27%)
  starting transfers between devices  69.3 us (19%)
  blocking collectives  47.8 us (13%)
  local copies, waits for them, and re-layouts  20.5 us (6%)
  other arithmetic  15.5 us (4%)
  loops' own time  7.87 us (2%)
    ppermute x16, waiting for transfers between devices, halo_rows(): before = lax.ppermute(last, axis, up)  97.9 us
    dot_general x64, matrix products, product(): jnp.einsum('ij,jc->ic', matrix, operand, precision=lax.Precision.HIGHEST)  53.2 us
    dot_general x64, matrix products, product(): jnp.einsum('rbj,ji->rbi', operand, matrix, precision=lax.Precision.HIGH)  47.2 us
    ppermute x16, starting transfers between devices, halo_rows(): before = lax.ppermute(last, axis, up)  38.5 us
    all_gather x1, blocking collectives, body(): volume = lax.all_gather(index_volume, 'depth', axis=0, tiled=True)  35.1 us
    ppermute x16, starting transfers between devices, halo_rows(): after = lax.ppermute(initial, axis, down)  30.7 us
    unnamed x1, blocking collectives  12.8 us
  transfers between devices with their start and end apart: 33, of which 33 were waited for; matrix products, arithmetic and copies ran while one was open for 4% of the time, Pallas kernels for 0%

commit v1 on v0

--- a/solution.py
+++ b/solution.py
@@ -106,7 +106,8 @@
     total_rows = height * lax.axis_size("row")
     angle_count = angles.shape[0]
     angle_no = section_no % angle_count
-    volume = lax.all_gather(index_volume, "depth", axis=0, tiled=True)
+    sent = jnp.stack([index_volume] * lax.axis_size("depth"))
+    volume = jnp.concatenate(lax.all_to_all(sent, "depth", 0, 0), axis=0)
     shifts = lax.all_gather(offsets, "depth", axis=0, tiled=True)
     layers = volume.shape[0]
     intensity = lax.dynamic_index_in_dim(measured, angle_no, 0, keepdims=False).astype(jnp.float32)

time: 370 us -> 347 us (0.938)
  blocking collectives: 47.8 us -> 13.9 us
  starting transfers between devices: 69.3 us -> 78.1 us
    all_gather x1 -> x0, blocking collectives: 35.1 us -> none  [body(): volume = lax.all_gather(index_volume, 'depth', axis=0, tiled=True)]
    all_to_all x0 -> x1, starting transfers between devices: none -> 6.03 us  [body(): volume = jnp.concatenate(lax.all_to_all(sent, 'depth', 0, 0), axis=0)]
  transfers between devices with their start and end apart: 33 -> 34, of which waited for: 33 -> 33; matrix products, arithmetic and copies ran while one was open for 4% -> 6% of each run, Pallas kernels for 0% -> 0%
where the time goes in v1:
time: 347 us; the launch traced here: 345 us
  waiting for transfers between devices  102 us (29%)
  matrix products  102 us (29%)
  starting transfers between devices  78.1 us (23%)
  local copies, waits for them, and re-layouts  22.7 us (7%)
  other arithmetic  15.4 us (4%)
  blocking collectives  13.9 us (4%)
  loops' own time  8.43 us (2%)
    ppermute x16, waiting for transfers between devices, halo_rows(): before = lax.ppermute(last, axis, up)  95.2 us
    dot_general x64, matrix products, product(): jnp.einsum('ij,jc->ic', matrix, operand, precision=lax.Precision.HIGHEST)  55.3 us
    dot_general x64, matrix products, product(): jnp.einsum('rbj,ji->rbi', operand, matrix, precision=lax.Precision.HIGH)  47.2 us
    ppermute x16, starting transfers between devices, halo_rows(): before = lax.ppermute(last, axis, up)  38 us
    ppermute x16, starting transfers between devices, halo_rows(): after = lax.ppermute(initial, axis, down)  33.4 us
    unnamed x1, blocking collectives  13.9 us
    another operation x1, loops' own time, body(): adjoint, terms = lax.fori_loop(0, layers, backward_step, (adjoint, terms))  6.98 us
  transfers between devices with their start and end apart: 34, of which 33 were waited for; matrix products, arithmetic and copies ran while one was open for 6% of the time, Pallas kernels for 0%

profile of v1, /device:TPU:2, one launch (start us, length us, event | category | flops | bytes accessed | tf_op | source)
XLA Modules:
  0.0 344.9 jit_solution(6944586890772344438)
XLA Ops:
  0.0 1.7 stack.123
  1.7 6.0 %all-to-all-start = ((bf16[8,1,16,2048]{3,2,1,0:T(8,128)(2,1)}), bf16[8,1,16,2048]{3,2,1,0:T(8,128)(2,1)S(1)}, u32[]{:S(2)}, u32[]{:S(2)}) async-start(bf16[8,1,16,2048]{3,2,1,0:T(8,128)(2,1)} %stack.123), calls=%async_computation | async-start | bytes 1048576 | tf_op jit(solution)/shard_map/all_to_all | solution.py:110
  13.0 13.9 %all-reduce.2 = s32[8]{0:T(128)S(1)} all-reduce(s32[8]{0:T(128)S(1)} %dynamic-update-slice), channel_id=1, replica_groups=mesh['depth'=8,'row'=32] {'depth'}, use_global_device_ids=true, to_apply=%add.2 | all-reduce | flops 8 | bytes 64
  27.6 3.7 %sine_bitcast_fusion = (f32[8,16,2048]{2,1,0:T(8,128)S(1)}, f32[8,16,2048]{2,1,0:T(8,128)S(1)}) fusion(bf16[8,1,16,2048]{3,2,1,0:T(8,128)(2,1)S(1)} %all-to-all-done), kind=kLoop, calls=%fused_computation.254 | loop fusion | flops 524288 | bytes 2621440 | tf_op jit(solution)/shard_map/sin | solution.py:120
  31.3 157.0 %while.38 = (s32[]{:T(128)}, f32[2,16,2048]{2,1,0:T(8,128)S(1)}, f32[8,2,16,2048]{3,2,1,0:T(8,128)}, s32[8]{0:T(128)S(1)}, f32[8,16,2048]{2,1,0:T(8,128)S(1)}, /*index=5*/f32[8,16,2048]{2,1,0:T(8,128)S(1)}, s32[]{:T(128)}) while((s32[]{:T(128)}, f32[2,16,2048]{2,1,0:T(8,128)S(1)}, f32[8,2,16,2048]{3,2,1,0:T(8,128)}, ...), condition=%wide.region_1.2_spmd.clone.clone, body=%wide.region_0.1_spmd.clone.clone.sunk | while | flops 273272320 | bytes 14237897 | solution.py:131
  31.4 4.6 %collective-permute-start = (f32[2,14,2048]{2,1,0:T(8,128)S(1)}, f32[2,14,2048]{2,1,0:T(8,128)S(1)}, u32[]{:S(2)}, u32[]{:S(2)}) collective-permute-start(f32[2,14,2048]{2,1,0:T(8,128)S(1)} %get-tuple-element.655), channel_id=1, source_target_pairs={{1,0},{2,1},{3,2},{4,3},{5,4},{6,5},{7,6},{8,7},{9,8},{10,9},{11,1... | collective-permute-start | bytes 688136 | tf_op jit(solution)/shard_map/while/body/eval_jaxpr/ppermute | solution.py:24
  36.1 1.9 collective-permute-start.1
  40.0 6.2 %collective-permute-done.1 = f32[2,14,2048]{2,1,0:T(8,128)S(1)} collective-permute-done((f32[2,14,2048]{2,1,0:T(8,128)S(1)}, f32[2,14,2048]{2,1,0:T(8,128)S(1)}, u32[]{:S(2)}, u32[]{:S(2)}) %collective-permute-start.1) | collective-permute-done | bytes 229408 | tf_op jit(solution)/shard_map/while/body/eval_jaxpr/ppermute | solution.py:23
  53.7 1.9 collective-permute-start
  55.6 2.4 collective-permute-start.1
  59.5 5.9 %collective-permute-done.1 = f32[2,14,2048]{2,1,0:T(8,128)S(1)} collective-permute-done((f32[2,14,2048]{2,1,0:T(8,128)S(1)}, f32[2,14,2048]{2,1,0:T(8,128)S(1)}, u32[]{:S(2)}, u32[]{:S(2)}) %collective-permute-start.1) | collective-permute-done | bytes 229408 | tf_op jit(solution)/shard_map/while/body/eval_jaxpr/ppermute | solution.py:23
  73.0 1.9 collective-permute-start
  74.9 2.4 collective-permute-start.1
  78.8 5.9 %collective-permute-done.1 = f32[2,14,2048]{2,1,0:T(8,128)S(1)} collective-permute-done((f32[2,14,2048]{2,1,0:T(8,128)S(1)}, f32[2,14,2048]{2,1,0:T(8,128)S(1)}, u32[]{:S(2)}, u32[]{:S(2)}) %collective-permute-start.1) | collective-permute-done | bytes 229408 | tf_op jit(solution)/shard_map/while/body/eval_jaxpr/ppermute | solution.py:23
  92.2 1.9 collective-permute-start
  94.1 2.4 collective-permute-start.1
  98.0 5.9 %collective-permute-done.1 = f32[2,14,2048]{2,1,0:T(8,128)S(1)} collective-permute-done((f32[2,14,2048]{2,1,0:T(8,128)S(1)}, f32[2,14,2048]{2,1,0:T(8,128)S(1)}, u32[]{:S(2)}, u32[]{:S(2)}) %collective-permute-start.1) | collective-permute-done | bytes 229408 | tf_op jit(solution)/shard_map/while/body/eval_jaxpr/ppermute | solution.py:23
  111.5 1.9 collective-permute-start
  113.4 2.4 collective-permute-start.1
  117.3 5.9 %collective-permute-done.1 = f32[2,14,2048]{2,1,0:T(8,128)S(1)} collective-permute-done((f32[2,14,2048]{2,1,0:T(8,128)S(1)}, f32[2,14,2048]{2,1,0:T(8,128)S(1)}, u32[]{:S(2)}, u32[]{:S(2)}) %collective-permute-start.1) | collective-permute-done | bytes 229408 | tf_op jit(solution)/shard_map/while/body/eval_jaxpr/ppermute | solution.py:23
  130.7 1.9 collective-permute-start
  132.7 2.4 collective-permute-start.1
  136.5 5.9 %collective-permute-done.1 = f32[2,14,2048]{2,1,0:T(8,128)S(1)} collective-permute-done((f32[2,14,2048]{2,1,0:T(8,128)S(1)}, f32[2,14,2048]{2,1,0:T(8,128)S(1)}, u32[]{:S(2)}, u32[]{:S(2)}) %collective-permute-start.1) | collective-permute-done | bytes 229408 | tf_op jit(solution)/shard_map/while/body/eval_jaxpr/ppermute | solution.py:23
  150.0 1.9 collective-permute-start
  151.9 2.4 collective-permute-start.1
  155.8 5.9 %collective-permute-done.1 = f32[2,14,2048]{2,1,0:T(8,128)S(1)} collective-permute-done((f32[2,14,2048]{2,1,0:T(8,128)S(1)}, f32[2,14,2048]{2,1,0:T(8,128)S(1)}, u32[]{:S(2)}, u32[]{:S(2)}) %collective-permute-start.1) | collective-permute-done | bytes 229408 | tf_op jit(solution)/shard_map/while/body/eval_jaxpr/ppermute | solution.py:23
  169.2 1.9 collective-permute-start
  171.2 2.4 collective-permute-start.1
  175.0 5.9 %collective-permute-done.1 = f32[2,14,2048]{2,1,0:T(8,128)S(1)} collective-permute-done((f32[2,14,2048]{2,1,0:T(8,128)S(1)}, f32[2,14,2048]{2,1,0:T(8,128)S(1)}, u32[]{:S(2)}, u32[]{:S(2)}) %collective-permute-start.1) | collective-permute-done | bytes 229408 | tf_op jit(solution)/shard_map/while/body/eval_jaxpr/ppermute | solution.py:23
  189.6 147.8 %while.39 = (s32[]{:T(128)}, f32[2,16,2048]{2,1,0:T(8,128)S(1)}, f32[8,16,2048]{2,1,0:T(8,128)}, f32[8,16,2048]{2,1,0:T(8,128)S(1)}, s32[8]{0:T(128)S(1)}, /*ind...) while((s32[]{:T(128)}, f32[2,16,2048]{2,1,0:T(8,128)S(1)}, ...), condition=%wide.region_3.4_spmd.clone.clone, body=%wide.region_2.3_spmd.clone.clone.sunk | while | flops 272724864 | bytes 14156587 | solution.py:148
  193.1 1.9 collective-permute-start.2
  195.0 2.4 collective-permute-start.3
  198.9 5.9 %collective-permute-done.3 = f32[2,14,2048]{2,1,0:T(8,128)S(1)} collective-permute-done((f32[2,14,2048]{2,1,0:T(8,128)S(1)}, f32[2,14,2048]{2,1,0:T(8,128)S(1)}, u32[]{:S(2)}, u32[]{:S(2)}) %collective-permute-start.3) | collective-permute-done | bytes 229408 | tf_op jit(solution)/shard_map/while/body/eval_jaxpr/ppermute | solution.py:23
  205.9 2.0 fusion.246
  211.5 1.9 collective-permute-start.2
  213.5 2.4 collective-permute-start.3
  217.3 5.9 %collective-permute-done.3 = f32[2,14,2048]{2,1,0:T(8,128)S(1)} collective-permute-done((f32[2,14,2048]{2,1,0:T(8,128)S(1)}, f32[2,14,2048]{2,1,0:T(8,128)S(1)}, u32[]{:S(2)}, u32[]{:S(2)}) %collective-permute-start.3) | collective-permute-done | bytes 229408 | tf_op jit(solution)/shard_map/while/body/eval_jaxpr/ppermute | solution.py:23
  224.4 2.0 fusion.246
  230.0 1.9 collective-permute-start.2
  231.9 2.4 collective-permute-start.3
  235.8 5.9 %collective-permute-done.3 = f32[2,14,2048]{2,1,0:T(8,128)S(1)} collective-permute-done((f32[2,14,2048]{2,1,0:T(8,128)S(1)}, f32[2,14,2048]{2,1,0:T(8,128)S(1)}, u32[]{:S(2)}, u32[]{:S(2)}) %collective-permute-start.3) | collective-permute-done | bytes 229408 | tf_op jit(solution)/shard_map/while/body/eval_jaxpr/ppermute | solution.py:23
  242.9 2.0 fusion.246
  248.5 1.9 collective-permute-start.2
  250.4 2.4 collective-permute-start.3
  254.3 5.9 %collective-permute-done.3 = f32[2,14,2048]{2,1,0:T(8,128)S(1)} collective-permute-done((f32[2,14,2048]{2,1,0:T(8,128)S(1)}, f32[2,14,2048]{2,1,0:T(8,128)S(1)}, u32[]{:S(2)}, u32[]{:S(2)}) %collective-permute-start.3) | collective-permute-done | bytes 229408 | tf_op jit(solution)/shard_map/while/body/eval_jaxpr/ppermute | solution.py:23
  261.4 2.0 fusion.246
  267.0 1.9 collective-permute-start.2
  268.9 2.4 collective-permute-start.3
  272.8 5.9 %collective-permute-done.3 = f32[2,14,2048]{2,1,0:T(8,128)S(1)} collective-permute-done((f32[2,14,2048]{2,1,0:T(8,128)S(1)}, f32[2,14,2048]{2,1,0:T(8,128)S(1)}, u32[]{:S(2)}, u32[]{:S(2)}) %collective-permute-start.3) | collective-permute-done | bytes 229408 | tf_op jit(solution)/shard_map/while/body/eval_jaxpr/ppermute | solution.py:23
  279.9 2.0 fusion.246
  285.4 1.9 collective-permute-start.2
  287.4 2.4 collective-permute-start.3
  291.2 5.9 %collective-permute-done.3 = f32[2,14,2048]{2,1,0:T(8,128)S(1)} collective-permute-done((f32[2,14,2048]{2,1,0:T(8,128)S(1)}, f32[2,14,2048]{2,1,0:T(8,128)S(1)}, u32[]{:S(2)}, u32[]{:S(2)}) %collective-permute-start.3) | collective-permute-done | bytes 229408 | tf_op jit(solution)/shard_map/while/body/eval_jaxpr/ppermute | solution.py:23
  298.3 2.0 fusion.246
  303.9 1.9 collective-permute-start.2
  305.8 2.4 collective-permute-start.3
  309.7 5.9 %collective-permute-done.3 = f32[2,14,2048]{2,1,0:T(8,128)S(1)} collective-permute-done((f32[2,14,2048]{2,1,0:T(8,128)S(1)}, f32[2,14,2048]{2,1,0:T(8,128)S(1)}, u32[]{:S(2)}, u32[]{:S(2)}) %collective-permute-start.3) | collective-permute-done | bytes 229408 | tf_op jit(solution)/shard_map/while/body/eval_jaxpr/ppermute | solution.py:23
  316.8 2.0 fusion.246
  322.4 1.9 collective-permute-start.2
  324.3 2.4 collective-permute-start.3
  328.2 5.9 %collective-permute-done.3 = f32[2,14,2048]{2,1,0:T(8,128)S(1)} collective-permute-done((f32[2,14,2048]{2,1,0:T(8,128)S(1)}, f32[2,14,2048]{2,1,0:T(8,128)S(1)}, u32[]{:S(2)}, u32[]{:S(2)}) %collective-permute-start.3) | collective-permute-done | bytes 229408 | tf_op jit(solution)/shard_map/while/body/eval_jaxpr/ppermute | solution.py:23
  335.3 2.0 fusion.246
  338.9 4.4 %collective-permute-done.4 = f32[1,16,2048]{2,1,0:T(8,128)S(1)} collective-permute-done((f32[1,16,2048]{2,1,0:T(8,128)S(1)}, f32[1,16,2048]{2,1,0:T(8,128)S(1)}, u32[]{:S(2)}, u32[]{:S(2)}) %collective-permute-start.4) | collective-permute-done | bytes 131104 | tf_op jit(solution)/shard_map/ppermute | solution.py:153
  343.3 1.6 select_add_fusion
  (377 shorter events, 120.5 us)
Async XLA Ops:
  1.7 25.9 %all-to-all-start = ((bf16[8,1,16,2048]{3,2,1,0:T(8,128)(2,1)}), bf16[8,1,16,2048]{3,2,1,0:T(8,128)(2,1)S(1)}, u32[]{:S(2)}, u32[]{:S(2)}) async-start(bf16[8,1,16,2048]{3,2,1,0:T(8,128)(2,1)} %stack.123), calls=%async_computation | async-start | bytes 1048576 | tf_op jit(solution)/shard_map/all_to_all | solution.py:110
  31.3 157.1 %copy-start = (bf16[2,16,2048]{2,1,0:T(8,128)(2,1)S(1)}, bf16[2,16,2048]{2,1,0:T(8,128)(2,1)}, u32[]{:S(2)}) copy-start(bf16[2,16,2048]{2,1,0:T(8,128)(2,1)} %param.11) | copy-start | bytes 393220
  31.4 8.5 %collective-permute-start = (f32[2,14,2048]{2,1,0:T(8,128)S(1)}, f32[2,14,2048]{2,1,0:T(8,128)S(1)}, u32[]{:S(2)}, u32[]{:S(2)}) collective-permute-start(f32[2,14,2048]{2,1,0:T(8,128)S(1)} %get-tuple-element.655), channel_id=1, source_target_pairs={{1,0},{2,1},{3,2},{4,3},{5,4},{6,5},{7,6},{8,7},{9,8},{10,9},{11,1... | collective-permute-start | bytes 688136 | tf_op jit(solution)/shard_map/while/body/eval_jaxpr/ppermute | solution.py:24
  36.1 10.1 %collective-permute-start.1 = (f32[2,14,2048]{2,1,0:T(8,128)S(1)}, f32[2,14,2048]{2,1,0:T(8,128)S(1)}, u32[]{:S(2)}, u32[]{:S(2)}) collective-permute-start(f32[2,14,2048]{2,1,0:T(8,128)S(1)} %get-tuple-element.656), channel_id=1, source_target_pairs={{0,1},{1,2},{2,3},{3,4},{4,5},{5,6},{6,7},{7,8},{8,9},{9,10},{10,1... | collective-permute-start | bytes 688136 | tf_op jit(solution)/shard_map/while/body/eval_jaxpr/ppermute | solution.py:23
  53.7 5.8 %collective-permute-start = (f32[2,14,2048]{2,1,0:T(8,128)S(1)}, f32[2,14,2048]{2,1,0:T(8,128)S(1)}, u32[]{:S(2)}, u32[]{:S(2)}) collective-permute-start(f32[2,14,2048]{2,1,0:T(8,128)S(1)} %get-tuple-element.655), channel_id=1, source_target_pairs={{1,0},{2,1},{3,2},{4,3},{5,4},{6,5},{7,6},{8,7},{9,8},{10,9},{11,1... | collective-permute-start | bytes 688136 | tf_op jit(solution)/shard_map/while/body/eval_jaxpr/ppermute | solution.py:24
  55.6 9.8 %collective-permute-start.1 = (f32[2,14,2048]{2,1,0:T(8,128)S(1)}, f32[2,14,2048]{2,1,0:T(8,128)S(1)}, u32[]{:S(2)}, u32[]{:S(2)}) collective-permute-start(f32[2,14,2048]{2,1,0:T(8,128)S(1)} %get-tuple-element.656), channel_id=1, source_target_pairs={{0,1},{1,2},{2,3},{3,4},{4,5},{5,6},{6,7},{7,8},{8,9},{9,10},{10,1... | collective-permute-start | bytes 688136 | tf_op jit(solution)/shard_map/while/body/eval_jaxpr/ppermute | solution.py:23
  73.0 5.8 %collective-permute-start = (f32[2,14,2048]{2,1,0:T(8,128)S(1)}, f32[2,14,2048]{2,1,0:T(8,128)S(1)}, u32[]{:S(2)}, u32[]{:S(2)}) collective-permute-start(f32[2,14,2048]{2,1,0:T(8,128)S(1)} %get-tuple-element.655), channel_id=1, source_target_pairs={{1,0},{2,1},{3,2},{4,3},{5,4},{6,5},{7,6},{8,7},{9,8},{10,9},{11,1... | collective-permute-start | bytes 688136 | tf_op jit(solution)/shard_map/while/body/eval_jaxpr/ppermute | solution.py:24
  74.9 9.8 %collective-permute-start.1 = (f32[2,14,2048]{2,1,0:T(8,128)S(1)}, f32[2,14,2048]{2,1,0:T(8,128)S(1)}, u32[]{:S(2)}, u32[]{:S(2)}) collective-permute-start(f32[2,14,2048]{2,1,0:T(8,128)S(1)} %get-tuple-element.656), channel_id=1, source_target_pairs={{0,1},{1,2},{2,3},{3,4},{4,5},{5,6},{6,7},{7,8},{8,9},{9,10},{10,1... | collective-permute-start | bytes 688136 | tf_op jit(solution)/shard_map/while/body/eval_jaxpr/ppermute | solution.py:23
  92.2 5.8 %collective-permute-start = (f32[2,14,2048]{2,1,0:T(8,128)S(1)}, f32[2,14,2048]{2,1,0:T(8,128)S(1)}, u32[]{:S(2)}, u32[]{:S(2)}) collective-permute-start(f32[2,14,2048]{2,1,0:T(8,128)S(1)} %get-tuple-element.655), channel_id=1, source_target_pairs={{1,0},{2,1},{3,2},{4,3},{5,4},{6,5},{7,6},{8,7},{9,8},{10,9},{11,1... | collective-permute-start | bytes 688136 | tf_op jit(solution)/shard_map/while/body/eval_jaxpr/ppermute | solution.py:24
  94.1 9.8 %collective-permute-start.1 = (f32[2,14,2048]{2,1,0:T(8,128)S(1)}, f32[2,14,2048]{2,1,0:T(8,128)S(1)}, u32[]{:S(2)}, u32[]{:S(2)}) collective-permute-start(f32[2,14,2048]{2,1,0:T(8,128)S(1)} %get-tuple-element.656), channel_id=1, source_target_pairs={{0,1},{1,2},{2,3},{3,4},{4,5},{5,6},{6,7},{7,8},{8,9},{9,10},{10,1... | collective-permute-start | bytes 688136 | tf_op jit(solution)/shard_map/while/body/eval_jaxpr/ppermute | solution.py:23
  111.5 5.8 %collective-permute-start = (f32[2,14,2048]{2,1,0:T(8,128)S(1)}, f32[2,14,2048]{2,1,0:T(8,128)S(1)}, u32[]{:S(2)}, u32[]{:S(2)}) collective-permute-start(f32[2,14,2048]{2,1,0:T(8,128)S(1)} %get-tuple-element.655), channel_id=1, source_target_pairs={{1,0},{2,1},{3,2},{4,3},{5,4},{6,5},{7,6},{8,7},{9,8},{10,9},{11,1... | collective-permute-start | bytes 688136 | tf_op jit(solution)/shard_map/while/body/eval_jaxpr/ppermute | solution.py:24
  113.4 9.8 %collective-permute-start.1 = (f32[2,14,2048]{2,1,0:T(8,128)S(1)}, f32[2,14,2048]{2,1,0:T(8,128)S(1)}, u32[]{:S(2)}, u32[]{:S(2)}) collective-permute-start(f32[2,14,2048]{2,1,0:T(8,128)S(1)} %get-tuple-element.656), channel_id=1, source_target_pairs={{0,1},{1,2},{2,3},{3,4},{4,5},{5,6},{6,7},{7,8},{8,9},{9,10},{10,1... | collective-permute-start | bytes 688136 | tf_op jit(solution)/shard_map/while/body/eval_jaxpr/ppermute | solution.py:23
  130.7 5.8 %collective-permute-start = (f32[2,14,2048]{2,1,0:T(8,128)S(1)}, f32[2,14,2048]{2,1,0:T(8,128)S(1)}, u32[]{:S(2)}, u32[]{:S(2)}) collective-permute-start(f32[2,14,2048]{2,1,0:T(8,128)S(1)} %get-tuple-element.655), channel_id=1, source_target_pairs={{1,0},{2,1},{3,2},{4,3},{5,4},{6,5},{7,6},{8,7},{9,8},{10,9},{11,1... | collective-permute-start | bytes 688136 | tf_op jit(solution)/shard_map/while/body/eval_jaxpr/ppermute | solution.py:24
  132.7 9.8 %collective-permute-start.1 = (f32[2,14,2048]{2,1,0:T(8,128)S(1)}, f32[2,14,2048]{2,1,0:T(8,128)S(1)}, u32[]{:S(2)}, u32[]{:S(2)}) collective-permute-start(f32[2,14,2048]{2,1,0:T(8,128)S(1)} %get-tuple-element.656), channel_id=1, source_target_pairs={{0,1},{1,2},{2,3},{3,4},{4,5},{5,6},{6,7},{7,8},{8,9},{9,10},{10,1... | collective-permute-start | bytes 688136 | tf_op jit(solution)/shard_map/while/body/eval_jaxpr/ppermute | solution.py:23
  150.0 5.8 %collective-permute-start = (f32[2,14,2048]{2,1,0:T(8,128)S(1)}, f32[2,14,2048]{2,1,0:T(8,128)S(1)}, u32[]{:S(2)}, u32[]{:S(2)}) collective-permute-start(f32[2,14,2048]{2,1,0:T(8,128)S(1)} %get-tuple-element.655), channel_id=1, source_target_pairs={{1,0},{2,1},{3,2},{4,3},{5,4},{6,5},{7,6},{8,7},{9,8},{10,9},{11,1... | collective-permute-start | bytes 688136 | tf_op jit(solution)/shard_map/while/body/eval_jaxpr/ppermute | solution.py:24
  151.9 9.8 %collective-permute-start.1 = (f32[2,14,2048]{2,1,0:T(8,128)S(1)}, f32[2,14,2048]{2,1,0:T(8,128)S(1)}, u32[]{:S(2)}, u32[]{:S(2)}) collective-permute-start(f32[2,14,2048]{2,1,0:T(8,128)S(1)} %get-tuple-element.656), channel_id=1, source_target_pairs={{0,1},{1,2},{2,3},{3,4},{4,5},{5,6},{6,7},{7,8},{8,9},{9,10},{10,1... | collective-permute-start | bytes 688136 | tf_op jit(solution)/shard_map/while/body/eval_jaxpr/ppermute | solution.py:23
  169.2 5.8 %collective-permute-start = (f32[2,14,2048]{2,1,0:T(8,128)S(1)}, f32[2,14,2048]{2,1,0:T(8,128)S(1)}, u32[]{:S(2)}, u32[]{:S(2)}) collective-permute-start(f32[2,14,2048]{2,1,0:T(8,128)S(1)} %get-tuple-element.655), channel_id=1, source_target_pairs={{1,0},{2,1},{3,2},{4,3},{5,4},{6,5},{7,6},{8,7},{9,8},{10,9},{11,1... | collective-permute-start | bytes 688136 | tf_op jit(solution)/shard_map/while/body/eval_jaxpr/ppermute | solution.py:24
  171.2 9.8 %collective-permute-start.1 = (f32[2,14,2048]{2,1,0:T(8,128)S(1)}, f32[2,14,2048]{2,1,0:T(8,128)S(1)}, u32[]{:S(2)}, u32[]{:S(2)}) collective-permute-start(f32[2,14,2048]{2,1,0:T(8,128)S(1)} %get-tuple-element.656), channel_id=1, source_target_pairs={{0,1},{1,2},{2,3},{3,4},{4,5},{5,6},{6,7},{7,8},{8,9},{9,10},{10,1... | collective-permute-start | bytes 688136 | tf_op jit(solution)/shard_map/while/body/eval_jaxpr/ppermute | solution.py:23
  193.1 5.8 %collective-permute-start.2 = (f32[2,14,2048]{2,1,0:T(8,128)S(1)}, f32[2,14,2048]{2,1,0:T(8,128)S(1)}, u32[]{:S(2)}, u32[]{:S(2)}) collective-permute-start(f32[2,14,2048]{2,1,0:T(8,128)S(1)} %get-tuple-element.668), channel_id=1, source_target_pairs={{1,0},{2,1},{3,2},{4,3},{5,4},{6,5},{7,6},{8,7},{9,8},{10,9},{11,1... | collective-permute-start | bytes 688136 | tf_op jit(solution)/shard_map/while/body/eval_jaxpr/ppermute | solution.py:24
  195.0 9.8 %collective-permute-start.3 = (f32[2,14,2048]{2,1,0:T(8,128)S(1)}, f32[2,14,2048]{2,1,0:T(8,128)S(1)}, u32[]{:S(2)}, u32[]{:S(2)}) collective-permute-start(f32[2,14,2048]{2,1,0:T(8,128)S(1)} %get-tuple-element.669), channel_id=1, source_target_pairs={{0,1},{1,2},{2,3},{3,4},{4,5},{5,6},{6,7},{7,8},{8,9},{9,10},{10,1... | collective-permute-start | bytes 688136 | tf_op jit(solution)/shard_map/while/body/eval_jaxpr/ppermute | solution.py:23
  211.5 5.8 %collective-permute-start.2 = (f32[2,14,2048]{2,1,0:T(8,128)S(1)}, f32[2,14,2048]{2,1,0:T(8,128)S(1)}, u32[]{:S(2)}, u32[]{:S(2)}) collective-permute-start(f32[2,14,2048]{2,1,0:T(8,128)S(1)} %get-tuple-element.668), channel_id=1, source_target_pairs={{1,0},{2,1},{3,2},{4,3},{5,4},{6,5},{7,6},{8,7},{9,8},{10,9},{11,1... | collective-permute-start | bytes 688136 | tf_op jit(solution)/shard_map/while/body/eval_jaxpr/ppermute | solution.py:24
  213.5 9.8 %collective-permute-start.3 = (f32[2,14,2048]{2,1,0:T(8,128)S(1)}, f32[2,14,2048]{2,1,0:T(8,128)S(1)}, u32[]{:S(2)}, u32[]{:S(2)}) collective-permute-start(f32[2,14,2048]{2,1,0:T(8,128)S(1)} %get-tuple-element.669), channel_id=1, source_target_pairs={{0,1},{1,2},{2,3},{3,4},{4,5},{5,6},{6,7},{7,8},{8,9},{9,10},{10,1... | collective-permute-start | bytes 688136 | tf_op jit(solution)/shard_map/while/body/eval_jaxpr/ppermute | solution.py:23
  230.0 5.8 %collective-permute-start.2 = (f32[2,14,2048]{2,1,0:T(8,128)S(1)}, f32[2,14,2048]{2,1,0:T(8,128)S(1)}, u32[]{:S(2)}, u32[]{:S(2)}) collective-permute-start(f32[2,14,2048]{2,1,0:T(8,128)S(1)} %get-tuple-element.668), channel_id=1, source_target_pairs={{1,0},{2,1},{3,2},{4,3},{5,4},{6,5},{7,6},{8,7},{9,8},{10,9},{11,1... | collective-permute-start | bytes 688136 | tf_op jit(solution)/shard_map/while/body/eval_jaxpr/ppermute | solution.py:24
  231.9 9.8 %collective-permute-start.3 = (f32[2,14,2048]{2,1,0:T(8,128)S(1)}, f32[2,14,2048]{2,1,0:T(8,128)S(1)}, u32[]{:S(2)}, u32[]{:S(2)}) collective-permute-start(f32[2,14,2048]{2,1,0:T(8,128)S(1)} %get-tuple-element.669), channel_id=1, source_target_pairs={{0,1},{1,2},{2,3},{3,4},{4,5},{5,6},{6,7},{7,8},{8,9},{9,10},{10,1... | collective-permute-start | bytes 688136 | tf_op jit(solution)/shard_map/while/body/eval_jaxpr/ppermute | solution.py:23
  248.5 5.8 %collective-permute-start.2 = (f32[2,14,2048]{2,1,0:T(8,128)S(1)}, f32[2,14,2048]{2,1,0:T(8,128)S(1)}, u32[]{:S(2)}, u32[]{:S(2)}) collective-permute-start(f32[2,14,2048]{2,1,0:T(8,128)S(1)} %get-tuple-element.668), channel_id=1, source_target_pairs={{1,0},{2,1},{3,2},{4,3},{5,4},{6,5},{7,6},{8,7},{9,8},{10,9},{11,1... | collective-permute-start | bytes 688136 | tf_op jit(solution)/shard_map/while/body/eval_jaxpr/ppermute | solution.py:24
  250.4 9.8 %collective-permute-start.3 = (f32[2,14,2048]{2,1,0:T(8,128)S(1)}, f32[2,14,2048]{2,1,0:T(8,128)S(1)}, u32[]{:S(2)}, u32[]{:S(2)}) collective-permute-start(f32[2,14,2048]{2,1,0:T(8,128)S(1)} %get-tuple-element.669), channel_id=1, source_target_pairs={{0,1},{1,2},{2,3},{3,4},{4,5},{5,6},{6,7},{7,8},{8,9},{9,10},{10,1... | collective-permute-start | bytes 688136 | tf_op jit(solution)/shard_map/while/body/eval_jaxpr/ppermute | solution.py:23
  267.0 5.8 %collective-permute-start.2 = (f32[2,14,2048]{2,1,0:T(8,128)S(1)}, f32[2,14,2048]{2,1,0:T(8,128)S(1)}, u32[]{:S(2)}, u32[]{:S(2)}) collective-permute-start(f32[2,14,2048]{2,1,0:T(8,128)S(1)} %get-tuple-element.668), channel_id=1, source_target_pairs={{1,0},{2,1},{3,2},{4,3},{5,4},{6,5},{7,6},{8,7},{9,8},{10,9},{11,1... | collective-permute-start | bytes 688136 | tf_op jit(solution)/shard_map/while/body/eval_jaxpr/ppermute | solution.py:24
  268.9 9.8 %collective-permute-start.3 = (f32[2,14,2048]{2,1,0:T(8,128)S(1)}, f32[2,14,2048]{2,1,0:T(8,128)S(1)}, u32[]{:S(2)}, u32[]{:S(2)}) collective-permute-start(f32[2,14,2048]{2,1,0:T(8,128)S(1)} %get-tuple-element.669), channel_id=1, source_target_pairs={{0,1},{1,2},{2,3},{3,4},{4,5},{5,6},{6,7},{7,8},{8,9},{9,10},{10,1... | collective-permute-start | bytes 688136 | tf_op jit(solution)/shard_map/while/body/eval_jaxpr/ppermute | solution.py:23
  285.4 5.8 %collective-permute-start.2 = (f32[2,14,2048]{2,1,0:T(8,128)S(1)}, f32[2,14,2048]{2,1,0:T(8,128)S(1)}, u32[]{:S(2)}, u32[]{:S(2)}) collective-permute-start(f32[2,14,2048]{2,1,0:T(8,128)S(1)} %get-tuple-element.668), channel_id=1, source_target_pairs={{1,0},{2,1},{3,2},{4,3},{5,4},{6,5},{7,6},{8,7},{9,8},{10,9},{11,1... | collective-permute-start | bytes 688136 | tf_op jit(solution)/shard_map/while/body/eval_jaxpr/ppermute | solution.py:24
  287.4 9.8 %collective-permute-start.3 = (f32[2,14,2048]{2,1,0:T(8,128)S(1)}, f32[2,14,2048]{2,1,0:T(8,128)S(1)}, u32[]{:S(2)}, u32[]{:S(2)}) collective-permute-start(f32[2,14,2048]{2,1,0:T(8,128)S(1)} %get-tuple-element.669), channel_id=1, source_target_pairs={{0,1},{1,2},{2,3},{3,4},{4,5},{5,6},{6,7},{7,8},{8,9},{9,10},{10,1... | collective-permute-start | bytes 688136 | tf_op jit(solution)/shard_map/while/body/eval_jaxpr/ppermute | solution.py:23
  303.9 5.8 %collective-permute-start.2 = (f32[2,14,2048]{2,1,0:T(8,128)S(1)}, f32[2,14,2048]{2,1,0:T(8,128)S(1)}, u32[]{:S(2)}, u32[]{:S(2)}) collective-permute-start(f32[2,14,2048]{2,1,0:T(8,128)S(1)} %get-tuple-element.668), channel_id=1, source_target_pairs={{1,0},{2,1},{3,2},{4,3},{5,4},{6,5},{7,6},{8,7},{9,8},{10,9},{11,1... | collective-permute-start | bytes 688136 | tf_op jit(solution)/shard_map/while/body/eval_jaxpr/ppermute | solution.py:24
  305.8 9.8 %collective-permute-start.3 = (f32[2,14,2048]{2,1,0:T(8,128)S(1)}, f32[2,14,2048]{2,1,0:T(8,128)S(1)}, u32[]{:S(2)}, u32[]{:S(2)}) collective-permute-start(f32[2,14,2048]{2,1,0:T(8,128)S(1)} %get-tuple-element.669), channel_id=1, source_target_pairs={{0,1},{1,2},{2,3},{3,4},{4,5},{5,6},{6,7},{7,8},{8,9},{9,10},{10,1... | collective-permute-start | bytes 688136 | tf_op jit(solution)/shard_map/while/body/eval_jaxpr/ppermute | solution.py:23
  322.4 5.8 %collective-permute-start.2 = (f32[2,14,2048]{2,1,0:T(8,128)S(1)}, f32[2,14,2048]{2,1,0:T(8,128)S(1)}, u32[]{:S(2)}, u32[]{:S(2)}) collective-permute-start(f32[2,14,2048]{2,1,0:T(8,128)S(1)} %get-tuple-element.668), channel_id=1, source_target_pairs={{1,0},{2,1},{3,2},{4,3},{5,4},{6,5},{7,6},{8,7},{9,8},{10,9},{11,1... | collective-permute-start | bytes 688136 | tf_op jit(solution)/shard_map/while/body/eval_jaxpr/ppermute | solution.py:24
  324.3 9.8 %collective-permute-start.3 = (f32[2,14,2048]{2,1,0:T(8,128)S(1)}, f32[2,14,2048]{2,1,0:T(8,128)S(1)}, u32[]{:S(2)}, u32[]{:S(2)}) collective-permute-start(f32[2,14,2048]{2,1,0:T(8,128)S(1)} %get-tuple-element.669), channel_id=1, source_target_pairs={{0,1},{1,2},{2,3},{3,4},{4,5},{5,6},{6,7},{7,8},{8,9},{9,10},{10,1... | collective-permute-start | bytes 688136 | tf_op jit(solution)/shard_map/while/body/eval_jaxpr/ppermute | solution.py:23
  338.3 5.1 %collective-permute-start.4 = (f32[1,16,2048]{2,1,0:T(8,128)S(1)}, f32[1,16,2048]{2,1,0:T(8,128)S(1)}, u32[]{:S(2)}, u32[]{:S(2)}) collective-permute-start(f32[1,16,2048]{2,1,0:T(8,128)S(1)} %constant_dynamic-slice_fusion), channel_id=1, source_target_pairs={{0,32},{32,0},{64,96},{96,64},{128,160},{160,128},{192,224},{224,1... | collective-permute-start | bytes 393224 | tf_op jit(solution)/shard_map/ppermute | solution.py:153
